TPU v7x, 256 devices: a whole 4x4x8 slice. The times are simulated.
256 devices in a mesh: row: 16 (over y, x), col: 16 (over z, core).
Axes of the slice: x: 4, y: 4, z: 8, core: 2. Of those that a mesh axis runs over, the one named last changes fastest.
Arguments:
- matrix: float32 [20480, 8, 2048], P('row', None, 'col'), may hold values from -36 to 36, as said below
Outputs:
- factors: float32 [20480, 8, 2048], P('row', None, 'col')
- upper: float32 [256, 8, 2048], P(None, None, 'col')
Inputs may be any that keep to these rules, and one draw needn't show every extreme that they name: A dense real matrix of full column rank.
All inputs are finite; a program needn't handle non-finite values.
Results may differ from a plain program's by a relative error of at most 0.0003.
Values sent between devices are 32-bit elements; how exact they have to be, the bound alone decides.
No kernel may reach another device: no remote copies, remote signals or barrier semaphores. Data moves between devices by JAX's collectives and lax.ppermute only.
A program may use at most 64 MiB of HBM per device.

v0:
```python
import math
import jax
import jax.numpy as jnp
from jax import lax
from jax.sharding import PartitionSpec as P


def spread(array, axis, root):
    mine = lax.axis_index(axis) == root
    return lax.psum(jnp.where(mine, array, jnp.zeros_like(array)), axis)


def upper_factor(gram):
    size = gram.shape[0]
    places = jnp.arange(size)

    def turn(j, carry):
        rest, lower = carry
        unit = (places == j).astype(gram.dtype)
        column = jnp.sum(rest * unit[None, :], axis=1)
        pivot = jnp.sqrt(jnp.sum(column * unit))
        column = jnp.where(places >= j, column / pivot, jnp.zeros_like(column))
        rest = rest - column[:, None] * column[None, :]
        lower = lower + column[:, None] * unit[None, :]
        return (rest, lower)

    rest, lower = lax.fori_loop(0, size, turn, (gram, jnp.zeros_like(gram)))
    return lower.T


def upper_inverse(factor):
    size = factor.shape[0]
    places = jnp.arange(size)

    def turn(step, inverse):
        j = size - 1 - step
        unit = (places == j).astype(factor.dtype)
        row_vals = jnp.sum(factor * unit[:, None], axis=0)
        pivot = jnp.sum(row_vals * unit)
        new_row = (unit - jnp.sum(row_vals[:, None] * inverse, axis=0)) / pivot
        return inverse + unit[:, None] * new_row[None, :]

    return lax.fori_loop(0, size, turn, jnp.zeros_like(factor))


def orthonormal(panel_rows):
    highest = lax.Precision.HIGHEST
    gram = jnp.dot(panel_rows.T, panel_rows, precision=highest, preferred_element_type=jnp.float32)
    factor = upper_factor(lax.psum(gram, "row"))
    return jnp.dot(
        panel_rows, upper_inverse(factor), precision=highest, preferred_element_type=jnp.float32
    )


def basis_for(block, spare, owner):
    source = jnp.where(lax.axis_index("col") == owner, block, spare)
    return spread(orthonormal(source), "col", owner)


def project(basis, work):
    local = jnp.einsum(
        "rp,rbc->pbc",
        basis,
        work,
        precision=lax.Precision.HIGHEST,
        preferred_element_type=jnp.float32,
    )
    return lax.psum(local, "row")


def remove(work, basis, coeffs):
    return work - jnp.einsum(
        "rp,pbc->rbc",
        basis,
        coeffs,
        precision=lax.Precision.HIGHEST,
        preferred_element_type=jnp.float32,
    )


def shards(matrix):
    scale = math.sqrt(matrix.shape[0] * lax.axis_size("row"))
    spare = matrix[:, 0, :]
    first = basis_for(matrix[:, 0, :], spare, 0)
    coef_one = project(first, matrix)
    middle = remove(matrix, first, coef_one)
    second = basis_for(middle[:, 0, :], spare, 1)
    coef_two = project(second, middle)
    final = remove(middle, second, coef_two)
    column = lax.axis_index("col")
    lead_block = jnp.where(
        column == 0, first * scale, jnp.where(column == 1, second * scale, final[:, 0, :])
    )
    factors = jnp.concatenate([lead_block[:, None, :], final[:, 1:, :]], axis=1)
    upper = jnp.concatenate([coef_one, coef_two], axis=0) / scale
    return (factors, upper)


def solution(mesh):
    in_specs = (P("row", None, "col"),)
    out_specs = (P("row", None, "col"), P(None, None, "col"))
    return jax.shard_map(shards, mesh=mesh, in_specs=in_specs, out_specs=out_specs, check_vma=False)
```

profile of v0, /device:TPU:32, one launch (start us, length us, event | category | flops | bytes accessed | tf_op | source)
XLA Modules:
  0.0 2057.3 jit_solution(17769544021011634935)
XLA Ops:
  7.2 6.2 copy.3
  13.4 2.6 fusion.26
  16.1 93.7 %all-reduce.7.cloned.1.call-done = f32[128,128]{1,0:T(8,128)} async-done(((f32[128,128]{1,0:T(8,128)}), f32[128,128]{1,0:T(8,128)}) %all-reduce.7.cloned.1.call-update) | async-done | bytes 65552 | tf_op jit(solution)/shard_map/psum | solution.py:49
  109.9 488.9 %while.64 = (s32[]{:T(128)}, f32[128,128]{1,0:T(8,128)}, f32[128,128]{1,0:T(8,128)S(1)}, s32[]{:T(128)}, s32[]{:T(128)}) while((s32[]{:T(128)}, f32[128,128]{1,0:T(8,128)}, f32[128,128]{1,0:T(8,128)S(1)}, s32[]{:T(128)}, s32[]{:T(128)}) %tuple.132), condition=%wide.region_4.5_spmd.clone.clone, body=%wide.region_1.4_spmd.clone.clone.sunk | while | flops 115586 | bytes 331883 | solution.py:27
  598.8 203.2 %while.62 = (s32[]{:T(128)}, f32[128,128]{1,0:T(8,128)S(1)}, f32[128,128]{1,0:T(8,128)S(1)}, s32[]{:T(128)}, s32[]{:T(128)}, /*index=5*/s32[]{:T(128)}) while((s32[]{:T(128)}, f32[128,128]{1,0:T(8,128)S(1)}, f32[128,128]{1,0:T(8,128)S(1)}, s32[]{:T(128)}, s32[]{:T(128)}, /*index=5*/s32[]{:T(128)}) %tuple.135), condition=%wide.region_9.10_spmd.clone, body=%wide.region_5.9_spmd.clone.sunk | while | flops 131971 | bytes 267384 | solution.py:43
  802.1 2.6 fusion.12
  804.8 107.2 %all-reduce.9.cloned.1.call-done = f32[1280,128]{0,1:T(8,128)} async-done(((f32[1280,128]{0,1:T(8,128)}), f32[1280,128]{0,1:T(8,128)}) %all-reduce.9.cloned.1.call-update) | async-done | bytes 655376 | tf_op jit(solution)/shard_map/psum | solution.py:10
  912.0 8.9 fusion.21
  921.0 98.3 %all-reduce.11.cloned.1.call-done = f32[128,8,128]{2,0,1:T(8,128)} async-done(((f32[128,8,128]{2,0,1:T(8,128)}), f32[128,8,128]{2,0,1:T(8,128)}) %all-reduce.11.cloned.1.call-update) | async-done | bytes 524304 | tf_op jit(solution)/shard_map/psum | solution.py:68
  1019.3 7.4 convolution_subtract_fusion.1
  1026.7 2.3 copy-done
  1029.0 2.6 fusion.19
  1032.0 90.3 %all-reduce.13.cloned.1.call-done = f32[128,128]{1,0:T(8,128)} async-done(((f32[128,128]{1,0:T(8,128)}), f32[128,128]{1,0:T(8,128)}) %all-reduce.13.cloned.1.call-update) | async-done | bytes 65552 | tf_op jit(solution)/shard_map/psum | solution.py:49
  1122.3 489.1 %while.65 = (s32[]{:T(128)}, f32[128,128]{1,0:T(8,128)}, f32[128,128]{1,0:T(8,128)S(1)}, s32[]{:T(128)}, s32[]{:T(128)}) while((s32[]{:T(128)}, f32[128,128]{1,0:T(8,128)}, f32[128,128]{1,0:T(8,128)S(1)}, s32[]{:T(128)}, s32[]{:T(128)}) %tuple.138), condition=%wide.region_16.17_spmd.clone.clone, body=%wide.region_13.16_spmd.clone.clone.sunk | while | flops 115586 | bytes 331883 | solution.py:27
  1128.4 1.6 select_add_fusion.5
  1611.5 203.2 %while.63 = (s32[]{:T(128)}, f32[128,128]{1,0:T(8,128)S(1)}, f32[128,128]{1,0:T(8,128)S(1)}, s32[]{:T(128)}, s32[]{:T(128)}, /*index=5*/s32[]{:T(128)}) while((s32[]{:T(128)}, f32[128,128]{1,0:T(8,128)S(1)}, f32[128,128]{1,0:T(8,128)S(1)}, s32[]{:T(128)}, s32[]{:T(128)}, /*index=5*/s32[]{:T(128)}) %tuple.141), condition=%wide.region_21.22_spmd.clone, body=%wide.region_17.21_spmd.clone.sunk | while | flops 131971 | bytes 267384 | solution.py:43
  1814.7 2.9 convolution_select_fusion
  1817.7 107.2 %all-reduce.15.cloned.1.call-done = f32[1280,128]{0,1:T(8,128)} async-done(((f32[1280,128]{0,1:T(8,128)}), f32[1280,128]{0,1:T(8,128)}) %all-reduce.15.cloned.1.call-update) | async-done | bytes 655376 | tf_op jit(solution)/shard_map/psum | solution.py:10
  1924.8 8.9 fusion.16
  1933.8 98.4 %all-reduce.17.cloned.1.call-done = f32[128,8,128]{2,0,1:T(8,128)} async-done(((f32[128,8,128]{2,0,1:T(8,128)}), f32[128,8,128]{2,0,1:T(8,128)}) %all-reduce.17.cloned.1.call-update) | async-done | bytes 524304 | tf_op jit(solution)/shard_map/psum | solution.py:68
  2032.2 7.0 convolution_subtract_fusion
  2039.7 2.7 pad_maximum_fusion
  2042.4 6.3 copy.14
  2048.9 1.6 copy.15
  (2845 shorter events, 1192.4 us)
Async XLA Ops:
  7.2 102.7 %all-reduce.7.cloned.1.call-start = ((), (), s32[]{:S(2)}) async-start(), calls=%async_computation | async-start | bytes 131072 | tf_op jit(solution)/shard_map/psum | solution.py:49
  16.1 895.9 %all-reduce.9.cloned.1.call-start = ((), (), s32[]{:S(2)}) async-start(), calls=%async_computation.1 | async-start | bytes 1310720 | tf_op jit(solution)/shard_map/psum | solution.py:10
  804.8 214.6 %all-reduce.11.cloned.1.call-start = ((), (), s32[]{:S(2)}) async-start(), calls=%async_computation.2 | async-start | bytes 1048576 | tf_op jit(solution)/shard_map/psum | solution.py:68
  912.0 107.3 %copy-start.1 = (f32[1280,128]{0,1:T(8,128)S(1)}, f32[1280,128]{0,1:T(8,128)}, u32[]{:S(2)}) copy-start(f32[1280,128]{0,1:T(8,128)} %all-reduce.9.cloned.1.call-done) | copy-start | bytes 1966084
  921.0 201.3 %all-reduce.13.cloned.1.call-start = ((), (), s32[]{:S(2)}) async-start(), calls=%async_computation.3 | async-start | bytes 131072 | tf_op jit(solution)/shard_map/psum | solution.py:49
  1026.7 2.3 copy-start
  1031.7 893.1 %all-reduce.15.cloned.1.call-start = ((), (), s32[]{:S(2)}) async-start(), calls=%async_computation.4 | async-start | bytes 1310720 | tf_op jit(solution)/shard_map/psum | solution.py:10
  1817.6 214.6 %all-reduce.17.cloned.1.call-start = ((), (), s32[]{:S(2)}) async-start(), calls=%async_computation.5 | async-start | bytes 1048576 | tf_op jit(solution)/shard_map/psum | solution.py:68
  1924.8 107.3 %copy-start.2 = (f32[1280,128]{0,1:T(8,128)S(1)}, f32[1280,128]{0,1:T(8,128)}, u32[]{:S(2)}) copy-start(f32[1280,128]{0,1:T(8,128)} %all-reduce.15.cloned.1.call-done) | copy-start | bytes 1966084
  2042.4 6.3 copy-start.3
  2042.4 6.3 copy-start.4
Sparse Core Ops, SparseCore 0:
  16.2 93.6 all-reduce.6
  804.9 107.0 all-reduce.8
  921.1 98.1 all-reduce.10
  1031.8 90.4 all-reduce.12
  1817.7 107.0 all-reduce.14
  1933.9 98.2 all-reduce.16
where the time goes:
time: 2090 us; the launch traced here: 2060 us
  other arithmetic  1200 us (57%)
  waiting for transfers between devices  595 us (28%)
  loops' own time  192 us (9%)
  matrix products  43 us (2%)
    add x256, other arithmetic, turn(): lower = lower + column[:, None] * unit[None, :]  398 us
    reduce_sum x256, other arithmetic, turn(): column = jnp.sum(rest * unit[None, :], axis=1)  241 us
    psum x2, waiting for transfers between devices, spread(): return lax.psum(jnp.where(mine, array, jnp.zeros_like(array)), axis)  214 us
    psum x2, waiting for transfers between devices, project(): return lax.psum(local, 'row')  197 us
    psum x2, waiting for transfers between devices, orthonormal(): factor = upper_factor(lax.psum(gram, 'row'))  184 us
    another operation x2, loops' own time, upper_factor(): rest, lower = lax.fori_loop(0, size, turn, (gram, jnp.zeros_like(gram)))  181 us
    div x256, other arithmetic, turn(): new_row = (unit - jnp.sum(row_vals[:, None] * inverse, axis=0)) / pivot  168 us
    reduce_sum x256, other arithmetic, turn(): pivot = jnp.sqrt(jnp.sum(column * unit))  157 us
  transfers between devices with their start and end apart: 6, of which 6 were waited for; matrix products, arithmetic and copies ran while one was open for 0% of the time, Pallas kernels for 0%

commit v1 on v0

--- a/solution.py
+++ b/solution.py
@@ -7,7 +7,7 @@
 
 def spread(array, axis, root):
     mine = lax.axis_index(axis) == root
-    return lax.psum(jnp.where(mine, array, jnp.zeros_like(array)), axis)
+    return jnp.sum(lax.all_gather(jnp.where(mine, array, jnp.zeros_like(array)), axis), 0)
 
 
 def upper_factor(gram):

time: 2090 us -> 2010 us (0.962)
  waiting for transfers between devices: 595 us -> 502 us
    psum x2 -> x0, waiting for transfers between devices: 214 us -> none  [spread(): return lax.psum(jnp.where(mine, array, jnp.zeros_like(array)), axis)]
    all_gather x0 -> x2, waiting for transfers between devices: none -> 127 us  [spread(): lax.all_gather(jnp.where(mine, array, jnp.zeros_like(array)), axis)]
where the time goes in v1:
time: 2010 us; the launch traced here: 1980 us
  other arithmetic  1200 us (60%)
  waiting for transfers between devices  502 us (25%)
  loops' own time  193 us (10%)
  matrix products  35.3 us (2%)
  local copies, waits for them, and re-layouts  30 us (1%)
    add x256, other arithmetic, turn(): lower = lower + column[:, None] * unit[None, :]  397 us
    reduce_sum x256, other arithmetic, turn(): column = jnp.sum(rest * unit[None, :], axis=1)  241 us
    psum x2, waiting for transfers between devices, project(): return lax.psum(local, 'row')  191 us
    psum x2, waiting for transfers between devices, orthonormal(): factor = upper_factor(lax.psum(gram, 'row'))  184 us
    another operation x2, loops' own time, upper_factor(): rest, lower = lax.fori_loop(0, size, turn, (gram, jnp.zeros_like(gram)))  182 us
    div x256, other arithmetic, turn(): new_row = (unit - jnp.sum(row_vals[:, None] * inverse, axis=0)) / pivot  168 us
    reduce_sum x256, other arithmetic, turn(): pivot = jnp.sqrt(jnp.sum(column * unit))  157 us
    reduce_sum x256, other arithmetic, turn(): pivot = jnp.sum(row_vals * unit)  156 us
  transfers between devices with their start and end apart: 6, of which 6 were waited for; matrix products, arithmetic and copies ran while one was open for 0% of the time, Pallas kernels for 0%

profile of v1, /device:TPU:32, one launch (start us, length us, event | category | flops | bytes accessed | tf_op | source)
XLA Modules:
  0.0 1978.2 jit_solution(2242054834089538467)
XLA Ops:
  7.2 3.5 copy.12
  10.7 2.3 copy-done.1
  15.1 93.7 %all-reduce.5.cloned.1.call-done = f32[128,128]{1,0:T(8,128)} async-done(((f32[128,128]{1,0:T(8,128)}), f32[128,128]{1,0:T(8,128)}) %all-reduce.5.cloned.1.call-update) | async-done | bytes 65552 | tf_op jit(solution)/shard_map/psum | solution.py:49
  108.8 489.4 %while.64 = (s32[]{:T(128)}, f32[128,128]{1,0:T(8,128)}, f32[128,128]{1,0:T(8,128)S(1)}, s32[]{:T(128)}, s32[]{:T(128)}) while((s32[]{:T(128)}, f32[128,128]{1,0:T(8,128)}, f32[128,128]{1,0:T(8,128)S(1)}, s32[]{:T(128)}, s32[]{:T(128)}) %tuple.135), condition=%wide.region_4.5_spmd.clone.clone, body=%wide.region_1.4_spmd.clone.clone.sunk | while | flops 115586 | bytes 331875 | solution.py:27
  598.3 203.0 %while.62 = (s32[]{:T(128)}, f32[128,128]{1,0:T(8,128)S(1)}, f32[128,128]{1,0:T(8,128)S(1)}, s32[]{:T(128)}, s32[]{:T(128)}, /*index=5*/s32[]{:T(128)}) while((s32[]{:T(128)}, f32[128,128]{1,0:T(8,128)S(1)}, f32[128,128]{1,0:T(8,128)S(1)}, s32[]{:T(128)}, s32[]{:T(128)}, /*index=5*/s32[]{:T(128)}) %tuple.138), condition=%wide.region_9.10_spmd.clone, body=%wide.region_5.9_spmd.clone.sunk | while | flops 131971 | bytes 267376 | solution.py:43
  801.3 2.7 fusion.12
  804.2 63.3 %all-gather.5.cloned.1.call-done = f32[20480,128]{0,1:T(8,128)} async-done(((f32[1280,128]{0,1:T(8,128)}), f32[20480,128]{0,1:T(8,128)}) %all-gather.5.cloned.1.call-update) | async-done | bytes 10485776 | tf_op jit(solution)/shard_map/all_gather | solution.py:10
  867.5 11.2 copy.26
  878.7 5.8 bitcast_reduce_fusion
  884.6 4.5 fusion.19
  889.4 95.6 %all-reduce.7.cloned.1.call-done = f32[128,8,128]{2,0,1:T(8,128)} async-done(((f32[128,8,128]{2,0,1:T(8,128)}), f32[128,8,128]{2,0,1:T(8,128)}) %all-reduce.7.cloned.1.call-update) | async-done | bytes 524304 | tf_op jit(solution)/shard_map/psum | solution.py:68
  984.9 7.7 convolution_subtract_fusion.1
  992.7 2.4 copy-done
  995.0 3.2 fusion.17
  998.3 90.5 %all-reduce.9.cloned.1.call-done = f32[128,128]{1,0:T(8,128)} async-done(((f32[128,128]{1,0:T(8,128)}), f32[128,128]{1,0:T(8,128)}) %all-reduce.9.cloned.1.call-update) | async-done | bytes 65552 | tf_op jit(solution)/shard_map/psum | solution.py:49
  1088.8 489.4 %while.65 = (s32[]{:T(128)}, f32[128,128]{1,0:T(8,128)}, f32[128,128]{1,0:T(8,128)S(1)}, s32[]{:T(128)}, s32[]{:T(128)}) while((s32[]{:T(128)}, f32[128,128]{1,0:T(8,128)}, f32[128,128]{1,0:T(8,128)S(1)}, s32[]{:T(128)}, s32[]{:T(128)}) %tuple.141), condition=%wide.region_16.17_spmd.clone.clone, body=%wide.region_13.16_spmd.clone.clone.sunk | while | flops 115586 | bytes 331875 | solution.py:27
  1578.3 203.0 %while.63 = (s32[]{:T(128)}, f32[128,128]{1,0:T(8,128)S(1)}, f32[128,128]{1,0:T(8,128)S(1)}, s32[]{:T(128)}, s32[]{:T(128)}, /*index=5*/s32[]{:T(128)}) while((s32[]{:T(128)}, f32[128,128]{1,0:T(8,128)S(1)}, f32[128,128]{1,0:T(8,128)S(1)}, s32[]{:T(128)}, s32[]{:T(128)}, /*index=5*/s32[]{:T(128)}) %tuple.144), condition=%wide.region_21.22_spmd.clone, body=%wide.region_17.21_spmd.clone.sunk | while | flops 131971 | bytes 267376 | solution.py:43
  1781.3 2.8 convolution_select_fusion
  1784.2 63.5 %all-gather.7.cloned.1.call-done = f32[20480,128]{1,0:T(8,128)} async-done(((f32[1280,128]{1,0:T(8,128)}), f32[20480,128]{1,0:T(8,128)}) %all-gather.7.cloned.1.call-update) | async-done | bytes 10485776 | tf_op jit(solution)/shard_map/all_gather | solution.py:10
  1847.7 4.5 reduce_sum.149
  1852.2 6.2 fusion.14
  1858.7 95.6 %all-reduce.11.cloned.1.call-done = f32[128,8,128]{2,0,1:T(8,128)} async-done(((f32[128,8,128]{2,0,1:T(8,128)}), f32[128,8,128]{2,0,1:T(8,128)}) %all-reduce.11.cloned.1.call-update) | async-done | bytes 524304 | tf_op jit(solution)/shard_map/psum | solution.py:68
  1954.3 6.3 convolution_subtract_fusion
  1961.4 8.3 copy.20
  (2852 shorter events, 1197.6 us)
Async XLA Ops:
  7.2 101.6 %all-reduce.5.cloned.1.call-start = ((), (), s32[]{:S(2)}) async-start(), calls=%async_computation | async-start | bytes 131072 | tf_op jit(solution)/shard_map/psum | solution.py:49
  10.7 2.4 copy-start.1
  15.0 852.5 %all-gather.5.cloned.1.call-start = ((), (), s32[]{:S(2)}) async-start(), calls=%async_computation.4 | async-start | bytes 11141120 | tf_op jit(solution)/shard_map/all_gather | solution.py:10
  803.9 80.6 %slice-start = ((s8[5242880]{0:T(1024)(128)(4,1)}), s8[1048576]{0:T(1024)(128)(4,1)S(1)}, s32[]{:S(2)}) async-start(s8[5242880]{0:T(1024)(128)(4,1)} %bitcast.46), calls=%async_computation.6 | async-start | bytes 2097152
  804.0 180.9 %all-reduce.7.cloned.1.call-start = ((), (), s32[]{:S(2)}) async-start(), calls=%async_computation.1 | async-start | bytes 1048576 | tf_op jit(solution)/shard_map/psum | solution.py:68
  867.5 17.0 slice-start.1
  889.1 199.7 %all-reduce.9.cloned.1.call-start = ((), (), s32[]{:S(2)}) async-start(), calls=%async_computation.2 | async-start | bytes 131072 | tf_op jit(solution)/shard_map/psum | solution.py:49
  992.7 2.4 copy-start
  998.2 849.4 %all-gather.7.cloned.1.call-start = ((), (), s32[]{:S(2)}) async-start(), calls=%async_computation.5 | async-start | bytes 11141120 | tf_op jit(solution)/shard_map/all_gather | solution.py:10
  1784.1 170.1 %all-reduce.11.cloned.1.call-start = ((), (), s32[]{:S(2)}) async-start(), calls=%async_computation.3 | async-start | bytes 1048576 | tf_op jit(solution)/shard_map/psum | solution.py:68
  1961.4 8.3 copy-start.2
  1961.4 8.3 copy-start.3
Sparse Core Ops, SparseCore 0:
  15.1 93.6 all-reduce.4
  804.1 63.3 all-gather.4
  889.2 95.6 all-reduce.6
  998.4 90.4 all-reduce.8
  1784.3 63.3 all-gather.6
  1858.6 95.6 all-reduce.10
